TPU v7x, 32 devices: a whole 2x2x4 slice. The times are simulated.
32 devices in a mesh: dp: 8 (over y, x, core), context: 4 (over z).
Axes of the slice: x: 2, y: 2, z: 4, core: 2. Of those that a mesh axis runs over, the one named last changes fastest.
Arguments:
- image_tokens: bfloat16 [8, 448, 3072], P('dp', 'context'), may hold values from -6 to 6
- text_tokens: bfloat16 [8, 64, 3072], P('dp', 'context'), may hold values from -6 to 6
- image_mod: bfloat16 [8, 3, 3072], P('dp'), may hold values from -4 to 4
- text_mod: bfloat16 [8, 3, 3072], P('dp'), may hold values from -4 to 4
- image_qkv_weight: bfloat16 [3072, 3, 16, 128], P('dp', None, 'context'), may hold values from -0.109375 to 0.109375
- text_qkv_weight: bfloat16 [3072, 3, 16, 128], P('dp', None, 'context'), may hold values from -0.109375 to 0.109375
- image_out_weight: bfloat16 [3072, 16, 128], P('dp', 'context'), may hold values from -1 to 1
- text_out_weight: bfloat16 [3072, 16, 128], P('dp', 'context'), may hold values from -1 to 1
- image_slope: bfloat16 [8, 448, 3072], P('dp', 'context'), may hold values from -0.119628906 to 0.119628906
- text_slope: bfloat16 [8, 64, 3072], P('dp', 'context'), may hold values from -0.119628906 to 0.119628906
Outputs:
- image_update: bfloat16 [8, 448, 3072], P('dp', 'context')
- text_update: bfloat16 [8, 64, 3072], P('dp', 'context')
- image_qkv_grad: float32 [3072, 3, 16, 128], P('dp', None, 'context')
- text_qkv_grad: float32 [3072, 3, 16, 128], P('dp', None, 'context')
- image_out_grad: float32 [3072, 16, 128], P('dp', 'context')
- text_out_grad: float32 [3072, 16, 128], P('dp', 'context')
- image_mod_grad: float32 [8, 3, 3072], P('dp')
- text_mod_grad: float32 [8, 3, 3072], P('dp')
All inputs are finite; a program needn't handle non-finite values.
Results may differ from a plain program's by a relative error of at most 0.015.
Values may be sent and summed in bfloat16 or wider, within the bound.
No kernel may reach another device: no remote copies, remote signals or barrier semaphores. Data moves between devices by JAX's collectives and lax.ppermute only.
A program may use at most 128 MiB of HBM per device.

v0:
```python
import jax
import jax.numpy as jnp
from jax import lax
from jax.sharding import PartitionSpec as P

norm_eps = 1e-06


def layer_normal(values):
    average = jnp.mean(values, axis=-1, keepdims=True)
    centred = values - average
    return centred * lax.rsqrt(jnp.mean(centred * centred, axis=-1, keepdims=True) + norm_eps)


def rms_normal(values):
    factor = lax.rsqrt(jnp.mean(values * values, axis=-1, keepdims=True) + norm_eps)
    return (values * factor, factor)


def rms_back(normed, factor, slopes):
    return factor * (slopes - normed * jnp.mean(slopes * normed, axis=-1, keepdims=True))


def modulate(tokens, modulation):
    normal = layer_normal(tokens.astype(jnp.float32))
    factors = modulation.astype(jnp.float32)
    return (normal, ((1.0 + factors[1]) * normal + factors[0]).astype(jnp.bfloat16))


def contract_rows(left_side, right_side):
    return lax.dot_general(
        left_side, right_side, (((0,), (0,)), ((), ())), preferred_element_type=jnp.float32
    )


def contract_last(left_side, right_side):
    return lax.dot_general(
        left_side, right_side, (((1,), (1,)), ((), ())), preferred_element_type=jnp.float32
    )


def body(
    image_tokens,
    text_tokens,
    image_mod,
    text_mod,
    image_qkv_weight,
    text_qkv_weight,
    image_out_weight,
    text_out_weight,
    image_slope,
    text_slope,
):
    groups = lax.axis_size("context")
    own_image = image_tokens.shape[1]
    own_text = text_tokens.shape[1]
    block_rows = own_image + own_text
    model_width = image_tokens.shape[2]
    shard_rows = image_qkv_weight.shape[0]
    head_count = image_qkv_weight.shape[2]
    head_size = image_qkv_weight.shape[3]
    inner_width = head_count * head_size
    triple = 3 * inner_width
    text_rows = own_text * groups
    score_scale = head_size ** (-0.5)
    whole_image, whole_text, slopes_image, slopes_text = (
        lax.all_gather(image_tokens, "context", axis=1, tiled=True),
        lax.all_gather(text_tokens, "context", axis=1, tiled=True),
        lax.all_gather(image_slope, "context", axis=1, tiled=True),
        lax.all_gather(text_slope, "context", axis=1, tiled=True),
    )
    full_q_image, full_q_text, full_o_image, full_o_text = (
        lax.all_gather(image_qkv_weight, "dp", axis=0, tiled=True),
        lax.all_gather(text_qkv_weight, "dp", axis=0, tiled=True),
        lax.all_gather(image_out_weight, "dp", axis=0, tiled=True),
        lax.all_gather(text_out_weight, "dp", axis=0, tiled=True),
    )
    wq_image = full_q_image.reshape(model_width, triple)
    wq_text = full_q_text.reshape(model_width, triple)
    wo_image = full_o_image.reshape(model_width, inner_width)
    wo_text = full_o_text.reshape(model_width, inner_width)
    normal_image, input_image = modulate(whole_image[0], image_mod[0])
    normal_text, input_text = modulate(whole_text[0], text_mod[0])
    projected = jnp.concatenate(
        [
            jnp.dot(input_text, wq_text, preferred_element_type=jnp.float32),
            jnp.dot(input_image, wq_image, preferred_element_type=jnp.float32),
        ],
        axis=0,
    )
    projected = projected.reshape(-1, 3, head_count, head_size)
    query_normal, query_factor = rms_normal(projected[:, 0])
    key_normal, key_factor = rms_normal(projected[:, 1])
    query_b = query_normal.astype(jnp.bfloat16)
    key_b = key_normal.astype(jnp.bfloat16)
    value_b = projected[:, 2].astype(jnp.bfloat16)
    scores = (
        jnp.einsum("ihe,jhe->hij", query_b, key_b, preferred_element_type=jnp.float32) * score_scale
    )
    raised = jnp.exp(scores)
    attn_probs = raised / jnp.sum(raised, axis=-1, keepdims=True)
    probs_b = attn_probs.astype(jnp.bfloat16)
    attended = jnp.einsum(
        "hij,jhe->ihe", probs_b, value_b, preferred_element_type=jnp.float32
    ).astype(jnp.bfloat16)
    flat_att = attended.reshape(-1, inner_width)
    att_text = flat_att[:text_rows]
    att_image = flat_att[text_rows:]
    blocks_text = att_text.reshape(groups, own_text, inner_width)
    blocks_image = att_image.reshape(groups, own_image, inner_width)
    block_count = block_rows * lax.axis_size("context") // block_rows
    part_text = blocks_text.reshape(block_count * own_text, inner_width)
    part_image = blocks_image.reshape(block_count * own_image, inner_width)
    out_text = contract_last(part_text, wo_text).reshape(block_count, own_text, model_width)
    out_image = contract_last(part_image, wo_image).reshape(block_count, own_image, model_width)
    mixed_rows = lax.psum_scatter(
        jnp.concatenate([out_text, out_image], axis=1)
        .reshape(block_rows * lax.axis_size("context"), model_width)
        .astype(jnp.bfloat16),
        "context",
        scatter_dimension=0,
        tiled=True,
    ).astype(jnp.float32)
    mixed_text = mixed_rows[:own_text]
    mixed_image = mixed_rows[own_text:]
    factors_image = image_mod[0].astype(jnp.float32)
    factors_text = text_mod[0].astype(jnp.float32)
    update_image = (factors_image[2] * mixed_image).astype(jnp.bfloat16)[None]
    update_text = (factors_text[2] * mixed_text).astype(jnp.bfloat16)[None]
    gate_part_image = jnp.sum(image_slope[0].astype(jnp.float32) * mixed_image, axis=0)
    gate_part_text = jnp.sum(text_slope[0].astype(jnp.float32) * mixed_text, axis=0)
    gated_image = (factors_image[2] * slopes_image[0].astype(jnp.float32)).astype(jnp.bfloat16)
    gated_text = (factors_text[2] * slopes_text[0].astype(jnp.float32)).astype(jnp.bfloat16)
    back_att = jnp.concatenate(
        [
            jnp.dot(gated_text, wo_text, preferred_element_type=jnp.float32),
            jnp.dot(gated_image, wo_image, preferred_element_type=jnp.float32),
        ],
        axis=0,
    )
    back_att = back_att.astype(jnp.bfloat16).reshape(-1, head_count, head_size)
    back_probs = jnp.einsum("ihe,jhe->hij", back_att, value_b, preferred_element_type=jnp.float32)
    back_value = jnp.einsum("hij,ihe->jhe", probs_b, back_att, preferred_element_type=jnp.float32)
    back_scores = (
        attn_probs
        * (back_probs - jnp.sum(attn_probs * back_probs, axis=-1, keepdims=True))
        * score_scale
    ).astype(jnp.bfloat16)
    back_query = jnp.einsum("hij,jhe->ihe", back_scores, key_b, preferred_element_type=jnp.float32)
    back_key = jnp.einsum("hij,ihe->jhe", back_scores, query_b, preferred_element_type=jnp.float32)
    back_qkv = (
        jnp.stack(
            [
                rms_back(query_normal, query_factor, back_query),
                rms_back(key_normal, key_factor, back_key),
                back_value,
            ],
            axis=1,
        )
        .reshape(-1, triple)
        .astype(jnp.bfloat16)
    )
    back_text = back_qkv[:text_rows]
    back_image = back_qkv[text_rows:]
    spread_image = contract_last(back_image, wq_image)
    spread_text = contract_last(back_text, wq_text)
    part_image = jnp.stack(
        [
            jnp.sum(spread_image, axis=0),
            jnp.sum(spread_image * normal_image, axis=0),
            gate_part_image,
        ]
    )
    part_text = jnp.stack(
        [jnp.sum(spread_text, axis=0), jnp.sum(spread_text * normal_text, axis=0), gate_part_text]
    )
    modsum_image, modsum_text = (
        lax.psum(part_image.astype(jnp.bfloat16), "context").astype(jnp.float32),
        lax.psum(part_text.astype(jnp.bfloat16), "context").astype(jnp.float32),
    )
    pieces = [contract_rows(input_image, back_image)]
    pieces.append(contract_rows(gated_image, att_image))
    pieces.append(contract_rows(gated_text, att_text))
    summed = lax.psum_scatter(
        jnp.concatenate(pieces, axis=1).astype(jnp.bfloat16), "dp", scatter_dimension=0, tiled=True
    ).astype(jnp.float32)
    grad_q_image = summed[:, :triple]
    remaining = summed[:, triple:]
    columns = lax.all_to_all(input_text[None], "dp", split_axis=2, concat_axis=0, tiled=True)
    slopes_all = lax.all_gather(back_text[None], "dp", axis=0, tiled=True)
    per_image = jnp.einsum("itd,itj->idj", columns, slopes_all, preferred_element_type=jnp.float32)
    rounded = lax.optimization_barrier(per_image.astype(jnp.bfloat16))
    grad_q_text = jnp.sum(rounded.astype(jnp.float32), axis=0)
    grad_o_image = remaining[:, :inner_width]
    grad_o_text = remaining[:, inner_width:]
    return (
        update_image,
        update_text,
        grad_q_image.reshape(shard_rows, 3, head_count, head_size),
        grad_q_text.reshape(shard_rows, 3, head_count, head_size),
        grad_o_image.reshape(shard_rows, head_count, head_size),
        grad_o_text.reshape(shard_rows, head_count, head_size),
        modsum_image[None],
        modsum_text[None],
    )


def solution(mesh):
    placed = (
        P("dp", "context", None),
        P("dp", "context", None),
        P("dp", None, None),
        P("dp", None, None),
        P("dp", None, "context", None),
        P("dp", None, "context", None),
        P("dp", "context", None),
        P("dp", "context", None),
        P("dp", "context", None),
        P("dp", "context", None),
    )
    return jax.shard_map(
        body,
        mesh=mesh,
        in_specs=placed,
        out_specs=(
            P("dp", "context", None),
            P("dp", "context", None),
            P("dp", None, "context", None),
            P("dp", None, "context", None),
            P("dp", "context", None),
            P("dp", "context", None),
            P("dp", None, None),
            P("dp", None, None),
        ),
        check_vma=False,
    )
```

profile of v0, /device:TPU:0, one launch (start us, length us, event | category | flops | bytes accessed | tf_op | source)
XLA Modules:
  0.0 606.1 jit_solution(18341433870807146927)
XLA Ops:
  11.3 19.2 %all_gather.27 = bf16[1,64,3072]{2,1,0:T(8,128)(2,1)S(1)} all-gather(bf16[1,16,3072]{2,1,0:T(8,128)(2,1)S(1)} %copy-done.28), channel_id=1, replica_groups=mesh['dp'=8,'context'=4] {'context'}, dimensions={1}, use_global_device_ids=true | all-gather | bytes 491520 | tf_op jit(solution)/shard_map/all_gather | solution.py:68
  30.9 19.6 %all_gather.33 = bf16[1,64,3072]{2,1,0:T(8,128)(2,1)} all-gather(bf16[1,16,3072]{2,1,0:T(8,128)(2,1)S(1)} %copy-done.23), channel_id=1, replica_groups=mesh['dp'=8,'context'=4] {'context'}, dimensions={1}, use_global_device_ids=true | all-gather | bytes 491520 | tf_op jit(solution)/shard_map/all_gather | solution.py:70
  52.8 24.9 %all-gather.10.cloned.1.call-done = bf16[1,448,3072]{2,1,0:T(8,128)(2,1)} async-done(((bf16[1,112,3072]{2,1,0:T(8,128)(2,1)}), bf16[1,448,3072]{2,1,0:T(8,128)(2,1)}) %all-gather.10.cloned.1.call-update) | async-done | bytes 2752528 | tf_op jit(solution)/shard_map/all_gather | solution.py:67
  81.7 29.0 %all-gather.14.cloned.1.call-done = bf16[3072,4,128]{2,1,0:T(4,128)(2,1)} async-done(((bf16[384,4,128]{2,1,0:T(4,128)(2,1)}), bf16[3072,4,128]{2,1,0:T(4,128)(2,1)}) %all-gather.14.cloned.1.call-update) | async-done | bytes 3145744 | tf_op jit(solution)/shard_map/all_gather | solution.py:76
  118.2 26.6 %all-gather.16.cloned.1.call-done = bf16[3072,4,128]{2,1,0:T(4,128)(2,1)} async-done(((bf16[384,4,128]{2,1,0:T(4,128)(2,1)}), bf16[3072,4,128]{2,1,0:T(4,128)(2,1)}) %all-gather.16.cloned.1.call-update) | async-done | bytes 3145744 | tf_op jit(solution)/shard_map/all_gather | solution.py:75
  156.3 46.9 %all-gather.18.cloned.1.call-done = bf16[1,448,3072]{2,1,0:T(8,128)(2,1)} async-done(((bf16[1,112,3072]{2,1,0:T(8,128)(2,1)}), bf16[1,448,3072]{2,1,0:T(8,128)(2,1)}) %all-gather.18.cloned.1.call-update) | async-done | bytes 2752528 | tf_op jit(solution)/shard_map/all_gather | solution.py:69
  208.3 54.1 %all-gather.8.cloned.1.call-done = bf16[3072,3,4,128]{3,2,1,0:T(4,128)(2,1)} async-done(((bf16[384,3,4,128]{3,2,1,0:T(4,128)(2,1)}), bf16[3072,3,4,128]{3,2,1,0:T(4,128)(2,1)}) %all-gather.8.cloned.1.call-update) | async-done | bytes 9437200 | tf_op jit(solution)/shard_map/all_gather | solution.py:74
  262.4 16.2 %reshape.247 = bf16[3072,1536]{1,0:T(8,128)(2,1)} reshape(bf16[3072,3,4,128]{3,2,1,0:T(4,128)(2,1)} %all-gather.8.cloned.1.call-done) | data formatting | bytes 18874368 | tf_op jit(solution)/shard_map/reshape | solution.py:79
  284.0 38.9 %all-gather.12.cloned.1.call-done = bf16[3072,3,4,128]{3,2,1,0:T(4,128)(2,1)} async-done(((bf16[384,3,4,128]{3,2,1,0:T(4,128)(2,1)}), bf16[3072,3,4,128]{3,2,1,0:T(4,128)(2,1)}) %all-gather.12.cloned.1.call-update) | async-done | bytes 9437200 | tf_op jit(solution)/shard_map/all_gather | solution.py:73
  322.9 15.9 %reshape.248 = bf16[3072,1536]{1,0:T(8,128)(2,1)} reshape(bf16[3072,3,4,128]{3,2,1,0:T(4,128)(2,1)} %all-gather.12.cloned.1.call-done) | data formatting | bytes 18874368 | tf_op jit(solution)/shard_map/reshape | solution.py:78
  338.8 7.6 %fusion.21 = f32[448,1536]{1,0:T(8,128)S(1)} fusion(bf16[3072,1536]{1,0:T(8,128)(2,1)} %reshape.248, bf16[1,448,3072]{2,1,0:T(8,128)(2,1)S(1)} %copy-done.1, f32[3072]{0:T(1024)} %bitcast.215, f32[448]{0:T(512)} %add_rsqrt_fusion.2, f32[448]{0:T(512)S(1)} %broadcast_multiply_fusion.2, f32[3072]{0:T(1024)} %bitcast.213), kind=kOutput, calls=%fused_computation.37 | convolution fusion | flops 4236115968 | bytes 14970368 | tf_op jit(solution)/shard_map/dot_general | solution.py:87
  359.4 8.2 %fusion.46 = f32[512,4,128]{0,2,1:T(8,128)} fusion(f32[4,512,512]{1,2,0:T(8,128)} %fusion.80, f32[512,3,4,128]{0,3,2,1:T(8,128)S(1)} %bitcast.182, f32[512,4]{0,1:T(4,128)} %copy-done.30, f32[4,512,512]{1,2,0:T(8,128)} %copy-done.10, f32[4,512]{1,0:T(4,128)} %copy-done.35), kind=kOutput, calls=%fused_computation.58 | convolution fusion | flops 278399488 | bytes 18898944 | tf_op jit(solution)/shard_map/hij,ihe->jhe/dot_general | solution.py:150
  367.6 10.0 %multiply_reduce_fusion.2 = (f32[512,4]{0,1:T(4,128)}, f32[512,4]{0,1:T(4,128)}, f32[512,4,128]{0,2,1:T(8,128)}) fusion(f32[512,3,4,128]{0,3,2,1:T(8,128)S(1)} %bitcast.183, f32[512,4]{0,1:T(4,128)} %copy-done.30, f32[512,4,128]{0,2,1:T(8,128)} %fusion.46, f32[512,4]{0,1:T(4,128)} %copy-done.29, f32[4,512,512]{1,2,0:T(8,128)} %fusion.80, ...), kind=kOutput, calls=%fused_computation.74 | convolution fusion | flops 279968256 | bytes 22077440 | tf_op jit(solution)/shard_map/hij,jhe->ihe/dot_general | solution.py:149
  384.6 5.7 reshape.258
  390.3 5.8 reshape.259
  418.7 6.2 %convolution_convert_fusion = bf16[3072,1536]{0,1:T(8,128)(2,1)S(1)} fusion(bf16[448,1536]{0,1:T(8,128)(2,1)S(1)} %bitcast.202, bf16[1,448,3072]{2,1,0:T(8,128)(2,1)S(1)} %copy-done.2, f32[3072]{0:T(1024)S(1)} %bitcast.216, f32[448]{0:T(512)S(1)} %copy-done.38, f32[3072]{0:T(1024)S(1)} %bitcast.214, f32[448]{0:T(512)S(1)} %broadcast_multiply_fusion.2), kind=kOutput, calls=%fused_computation.3 | convolution fusion | flops 4240834560 | bytes 13594112 | tf_op jit(solution)/shard_map/dot_general | solution.py:31
  424.9 7.6 %pad_maximum_fusion = bf16[3072,2560]{0,1:T(8,128)(2,1)} fusion(bf16[3072,512]{0,1:T(8,128)(2,1)S(1)} %convolution_convert_fusion.2, bf16[3072,512]{0,1:T(8,128)(2,1)S(1)} %convolution_convert_fusion.3, bf16[3072,1536]{0,1:T(8,128)(2,1)S(1)} %convolution_convert_fusion), kind=kLoop, calls=%fused_computation.2 | loop fusion | flops 47185920 | bytes 31457280 | tf_op jit(solution)/shard_map/concatenate | solution.py:185
  432.5 20.1 %copy.92 = bf16[3072,2560]{1,0:T(8,128)(2,1)} copy(bf16[3072,2560]{0,1:T(8,128)(2,1)} %pad_maximum_fusion) | data formatting | bytes 31457280
  457.0 18.9 %reduce.2 = bf16[3072,64]{1,0:T(8,128)(2,1)} reduce(bf16[3072,1,64]{2,1,0:T(2,128)(2,1)} %bitcast.193, bf16[]{:T(256)} %broadcast.209), dimensions={1}, to_apply=%bitcast.152.reduce_sub_computation | reduce | bytes 786434
  478.6 12.6 %all_to_all.18 = bf16[8,2,12288]{2,1,0:T(2,128)(2,1)} all-to-all(bf16[8,2,12288]{2,1,0:T(2,128)(2,1)} %reshape.268), channel_id=1, replica_groups=mesh['dp'=8,'context'=4] {'dp'}, dimensions={0} | all-to-all | bytes 786432 | tf_op jit(solution)/shard_map/all_to_all | solution.py:189
  500.1 7.3 %fusion.103 = (bf16[3072]{0:T(1024)(128)(2,1)S(1)}, bf16[3072]{0:T(1024)(128)(2,1)S(1)}) fusion(f32[64]{0:T(128)} %copy-done.37, f32[64]{0:T(128)} %copy-done.36, bf16[1,64,3072]{2,1,0:T(8,128)(2,1)S(1)} %all_gather.27, bf16[64,1536]{0,1:T(8,128)(2,1)S(1)} %bitcast.196, bf16[3072,1536]{1,0:T(8,128)(2,1)} %reshape.247), kind=kOutput, calls=%fused_computation.131 | convolution fusion | flops 605153280 | bytes 10039808 | tf_op jit(solution)/shard_map/dot_general | solution.py:37
  507.5 9.5 %fusion.102 = (bf16[3072]{0:T(1024)(128)(2,1)S(1)}, bf16[3072]{0:T(1024)(128)(2,1)S(1)}) fusion(f32[448]{0:T(512)S(1)} %copy-done.39, f32[448]{0:T(512)S(1)} %broadcast_multiply_fusion.2, bf16[1,448,3072]{2,1,0:T(8,128)(2,1)S(1)} %copy-done.2, bf16[448,1536]{0,1:T(8,128)(2,1)S(1)} %bitcast.203, bf16[3072,1536]{1,0:T(8,128)(2,1)} %reshape.248), kind=kOutput, calls=%fused_computation.130 | convolution fusion | flops 4236109824 | bytes 13581824 | tf_op jit(solution)/shard_map/dot_general | solution.py:37
  527.6 19.2 %all-reduce = (bf16[1,3,3072]{2,0,1:T(2,128)(2,1)S(1)}, bf16[1,3,3072]{2,0,1:T(2,128)(2,1)S(1)}) all-reduce(bf16[1,3,3072]{2,0,1:T(2,128)(2,1)S(1)} %broadcast_in_dim.37, bf16[1,3,3072]{2,0,1:T(2,128)(2,1)S(1)} %broadcast_in_dim.39), channel_id=1, replica_groups=mesh['dp'=8,'context'=4] {'context'}, use_global_device_ids=true, to_apply=%region_16.0 | all-reduce | flops 18432 | bytes 73728 | tf_op jit(solution)/shard_map/psum | solution.py:178
  548.1 39.9 %reduce-scatter.7.cloned.1.call-done = bf16[384,2560]{1,0:T(8,128)(2,1)} async-done(((bf16[3072,2560]{1,0:T(8,128)(2,1)}), bf16[384,2560]{1,0:T(8,128)(2,1)}) %reduce-scatter.7.cloned.1.call-update) | async-done | bytes 1966096
  (179 shorter events, 121.7 us)
Async XLA Ops:
  7.2 4.1 copy-start.27
  7.2 4.1 copy-start.28
  7.2 23.7 %copy-start.23 = (bf16[1,16,3072]{2,1,0:T(8,128)(2,1)S(1)}, bf16[1,16,3072]{2,1,0:T(8,128)(2,1)}, u32[]{:S(2)}) copy-start(bf16[1,16,3072]{2,1,0:T(8,128)(2,1)} %param.19) | copy-start | bytes 294916
  7.2 70.4 %all-gather.10.cloned.1.call-start = ((), (), s32[]{:S(2)}) async-start(), calls=%async_computation.4 | async-start | bytes 3440640 | tf_op jit(solution)/shard_map/all_gather | solution.py:67
  7.9 102.8 %all-gather.14.cloned.1.call-start = ((), (), s32[]{:S(2)}) async-start(), calls=%async_computation.6 | async-start | bytes 3538944 | tf_op jit(solution)/shard_map/all_gather | solution.py:76
  8.7 136.1 %all-gather.16.cloned.1.call-start = ((), (), s32[]{:S(2)}) async-start(), calls=%async_computation.7 | async-start | bytes 3538944 | tf_op jit(solution)/shard_map/all_gather | solution.py:75
  9.4 193.8 %all-gather.18.cloned.1.call-start = ((), (), s32[]{:S(2)}) async-start(), calls=%async_computation.9 | async-start | bytes 3440640 | tf_op jit(solution)/shard_map/all_gather | solution.py:69
  10.0 252.4 %all-gather.8.cloned.1.call-start = ((), (), s32[]{:S(2)}) async-start(), calls=%async_computation.3 | async-start | bytes 10616832 | tf_op jit(solution)/shard_map/all_gather | solution.py:74
  10.6 312.3 %all-gather.12.cloned.1.call-start = ((), (), s32[]{:S(2)}) async-start(), calls=%async_computation.5 | async-start | bytes 10616832 | tf_op jit(solution)/shard_map/all_gather | solution.py:73
  11.2 505.8 %all-gather.20.cloned.1.call-start = ((), (), s32[]{:S(2)}) async-start(), calls=%async_computation.10 | async-start | bytes 1769472 | tf_op jit(solution)/shard_map/all_gather | solution.py:190
  30.6 84.2 %copy-start.36 = (f32[64]{0:T(128)}, f32[64]{0:T(128)S(1)}, u32[]{:S(2)}) copy-start(f32[64]{0:T(128)S(1)} %broadcast_multiply_fusion.3) | copy-start | bytes 772
  50.5 64.4 %copy-start.37 = (f32[64]{0:T(128)}, f32[64]{0:T(128)S(1)}, u32[]{:S(2)}) copy-start(f32[64]{0:T(128)S(1)} %add_rsqrt_fusion.3) | copy-start | bytes 772
  208.3 70.3 %copy-start.4 = (bf16[1,64,3072]{2,1,0:T(8,128)(2,1)S(1)}, bf16[1,64,3072]{2,1,0:T(8,128)(2,1)}, u32[]{:S(2)}) copy-start(bf16[1,64,3072]{2,1,0:T(8,128)(2,1)} %fusion.63) | copy-start | bytes 1179652
  284.0 54.8 %copy-start.1 = (bf16[1,448,3072]{2,1,0:T(8,128)(2,1)S(1)}, bf16[1,448,3072]{2,1,0:T(8,128)(2,1)}, u32[]{:S(2)}) copy-start(bf16[1,448,3072]{2,1,0:T(8,128)(2,1)} %all-gather.10.cloned.1.call-done) | copy-start | bytes 8257540
  351.0 4.7 copy-start.29
  351.0 4.7 copy-start.30
  377.6 4.3 copy-start.16
  384.5 139.8 %reduce-scatter.5.cloned.1.call-start = ((), (), s32[]{:S(2)}) async-start(), calls=%async_computation.8 | async-start | bytes 3932160 | tf_op jit(solution)/shard_map/reduce_scatter | solution.py:116
  399.1 10.1 %copy-start.13 = (bf16[3072,512,1]{1,0,2:T(8,128)(2,1)S(1)}, bf16[3072,512,1]{1,0,2:T(8,128)(2,1)}, u32[]{:S(2)}) copy-start(bf16[3072,512,1]{1,0,2:T(8,128)(2,1)} %reshape.259) | copy-start | bytes 9437188
  414.1 173.9 %reduce-scatter.7.cloned.1.call-start = ((), (), s32[]{:S(2)}) async-start(), calls=%async_computation.11 | async-start | bytes 17694720
  475.9 24.2 %copy-start.11 = (bf16[64,3,4,128]{0,3,2,1:T(8,128)(2,1)S(1)}, bf16[64,3,4,128]{0,3,2,1:T(8,128)(2,1)}, u32[]{:S(2)}) copy-start(bf16[64,3,4,128]{0,3,2,1:T(8,128)(2,1)} %pad_maximum_fusion.5) | copy-start | bytes 589828
  500.1 7.3 %copy-start.20 = (bf16[448,3,4,128]{0,3,2,1:T(8,128)(2,1)S(1)}, bf16[448,3,4,128]{0,3,2,1:T(8,128)(2,1)}, u32[]{:S(2)}) copy-start(bf16[448,3,4,128]{0,3,2,1:T(8,128)(2,1)} %copy-done.19) | copy-start | bytes 4128772
  500.1 7.4 %copy-start.39 = (f32[448]{0:T(512)S(1)}, f32[448]{0:T(512)}, u32[]{:S(2)}) copy-start(f32[448]{0:T(512)} %add_rsqrt_fusion.2) | copy-start | bytes 5380
  507.4 9.6 %copy-start.18 = (bf16[1,64,8,384]{3,1,2,0:T(8,128)(2,1)S(1)}, bf16[1,64,8,384]{3,1,2,0:T(8,128)(2,1)}, u32[]{:S(2)}) copy-start(bf16[1,64,8,384]{3,1,2,0:T(8,128)(2,1)} %copy.74) | copy-start | bytes 1179652
  (26 other events, 59.3 us)
Sparse Core Ops, SparseCore 0:
  9.6 68.0 all-gather.9
  79.5 31.1 all-gather.13
  112.6 32.1 all-gather.15
  146.3 56.9 all-gather.17
  204.9 57.4 all-gather.7
  264.1 58.6 all-gather.11
  384.6 25.6 all-gather.19
  414.2 60.3 reduce-scatter.4
  478.1 109.8 reduce-scatter.6
where the time goes:
time: 612 us; the launch traced here: 606 us
  waiting for transfers between devices  264 us (43%)
  local copies, waits for them, and re-layouts  126 us (21%)
  matrix products  84.2 us (14%)
  blocking collectives  70.6 us (12%)
  other arithmetic  46.6 us (8%)
  between operations  14.7 us (2%)
    all_gather x1, waiting for transfers between devices, body(): lax.all_gather(text_qkv_weight, 'dp', axis=0, tiled=True)  54.1 us
    unnamed x93, local copies, waits for them, and re-layouts  51.8 us
    all_gather x1, waiting for transfers between devices, body(): lax.all_gather(image_slope, 'context', axis=1, tiled=True)  46.9 us
    unnamed x10, waiting for transfers between devices  43.6 us
    all_gather x1, waiting for transfers between devices, body(): lax.all_gather(image_qkv_weight, 'dp', axis=0, tiled=True)  38.9 us
    all_gather x1, waiting for transfers between devices, body(): lax.all_gather(text_out_weight, 'dp', axis=0, tiled=True)  29 us
    all_gather x1, waiting for transfers between devices, body(): lax.all_gather(image_out_weight, 'dp', axis=0, tiled=True)  26.6 us
    all_gather x1, waiting for transfers between devices, body(): lax.all_gather(image_tokens, 'context', axis=1, tiled=True)  24.9 us
  transfers between devices with their start and end apart: 9, of which 7 were waited for; matrix products, arithmetic and copies ran while one was open for 30% of the time, Pallas kernels for 0%

commit v1 on v0

--- a/solution.py
+++ b/solution.py
@@ -4,6 +4,24 @@
 from jax.sharding import PartitionSpec as P
 
 norm_eps = 1e-06
+
+
+def ring_gather(shard, axis, dim):
+    ways, here, hop = (lax.axis_size(axis), lax.axis_index(axis), shard.shape[dim])
+    lengths = [n * ways if d == dim else n for d, n in enumerate(shard.shape)]
+    full = lax.dynamic_update_slice_in_dim(
+        jnp.zeros(lengths, shard.dtype), shard, here * hop, axis=dim
+    )
+    going_up = going_down = shard
+    for far in range(1, ways // 2 + 1):
+        going_up = lax.ppermute(going_up, axis, [(d, (d + 1) % ways) for d in range(ways)])
+        full = lax.dynamic_update_slice_in_dim(full, going_up, (here - far) % ways * hop, axis=dim)
+        if 2 * far < ways:
+            going_down = lax.ppermute(going_down, axis, [(d, (d - 1) % ways) for d in range(ways)])
+            full = lax.dynamic_update_slice_in_dim(
+                full, going_down, (here + far) % ways * hop, axis=dim
+            )
+    return full
 
 
 def layer_normal(values):
@@ -66,7 +84,7 @@
     whole_image, whole_text, slopes_image, slopes_text = (
         lax.all_gather(image_tokens, "context", axis=1, tiled=True),
         lax.all_gather(text_tokens, "context", axis=1, tiled=True),
-        lax.all_gather(image_slope, "context", axis=1, tiled=True),
+        ring_gather(image_slope, "context", 1),
         lax.all_gather(text_slope, "context", axis=1, tiled=True),
     )
     full_q_image, full_q_text, full_o_image, full_o_text = (

time: 612 us -> 580 us (0.948)
  waiting for transfers between devices: 264 us -> 165 us
  blocking collectives: 70.6 us -> 124 us
  starting transfers between devices: 0.35 us -> 6.49 us
    all_gather x1, blocking collectives: 19.2 us -> 73.2 us  [body(): lax.all_gather(text_tokens, 'context', axis=1, tiled=True)]
    all_gather x1 -> x0, waiting for transfers between devices: 46.9 us -> none  [body(): lax.all_gather(image_slope, 'context', axis=1, tiled=True)]
    all_gather x1, waiting for transfers between devices: 29 us -> 3.57 us  [body(): lax.all_gather(text_out_weight, 'dp', axis=0, tiled=True)]
    all_gather x1, waiting for transfers between devices: 24.9 us -> 0.01 us  [body(): lax.all_gather(image_tokens, 'context', axis=1, tiled=True)]
    all_gather x1, waiting for transfers between devices: 54.1 us -> 43.8 us  [body(): lax.all_gather(text_qkv_weight, 'dp', axis=0, tiled=True)]
    ppermute x0 -> x3, waiting for transfers between devices: none -> 9.9 us  [the longest x2 9.9 us: ring_gather(): lax.ppermute(going_up, axis, [(d, (d + 1) % ways) for d in range(ways)])]
    ppermute x0 -> x3, starting transfers between devices: none -> 6.18 us  [the longest x1 5.13 us: ring_gather(): lax.ppermute(going_down, axis, [(d, (d - 1) % ways) for d in range(ways)])]
    unnamed x93 -> x91, local copies, waits for them, and re-layouts: 51.8 us -> 49.9 us
  transfers between devices with their start and end apart: 9 -> 11, of which waited for: 7 -> 6; matrix products, arithmetic and copies ran while one was open for 30% -> 33% of each run, Pallas kernels for 0% -> 0%
where the time goes in v1:
time: 580 us; the launch traced here: 574 us
  waiting for transfers between devices  165 us (28%)
  local copies, waits for them, and re-layouts  129 us (22%)
  blocking collectives  124 us (21%)
  matrix products  86.2 us (15%)
  other arithmetic  48.2 us (8%)
  between operations  15 us (3%)
  starting transfers between devices  6.49 us (1%)
    all_gather x1, blocking collectives, body(): lax.all_gather(text_tokens, 'context', axis=1, tiled=True)  73.2 us
    unnamed x91, local copies, waits for them, and re-layouts  49.9 us
    all_gather x1, waiting for transfers between devices, body(): lax.all_gather(text_qkv_weight, 'dp', axis=0, tiled=True)  43.8 us
    unnamed x9, waiting for transfers between devices  42 us
    all_gather x1, waiting for transfers between devices, body(): lax.all_gather(image_qkv_weight, 'dp', axis=0, tiled=True)  38.9 us
    all_gather x1, waiting for transfers between devices, body(): lax.all_gather(image_out_weight, 'dp', axis=0, tiled=True)  26.6 us
    dot_general x4, matrix products, contract_last(): lax.dot_general(left_side, right_side, (((1,), (1,)), ((), ())), preferre...  22.8 us
    psum x1, blocking collectives, body(): lax.psum(part_image.astype(jnp.bfloat16), 'context').astype(jnp.float32)  20.3 us
  transfers between devices with their start and end apart: 11, of which 6 were waited for; matrix products, arithmetic and copies ran while one was open for 33% of the time, Pallas kernels for 0%

profile of v1, /device:TPU:0, one launch (start us, length us, event | category | flops | bytes accessed | tf_op | source)
XLA Modules:
  0.0 573.6 jit_solution(9897960337860694268)
XLA Ops:
  17.3 73.2 %all_gather.24 = bf16[1,64,3072]{2,1,0:T(8,128)(2,1)S(1)} all-gather(bf16[1,16,3072]{2,1,0:T(8,128)(2,1)} %param.11), channel_id=1, replica_groups=mesh['dp'=8,'context'=4] {'context'}, dimensions={1}, use_global_device_ids=true | all-gather | bytes 491520 | tf_op jit(solution)/shard_map/all_gather | solution.py:86
  90.9 17.7 %all_gather.30 = bf16[1,64,3072]{2,1,0:T(8,128)(2,1)} all-gather(bf16[1,16,3072]{2,1,0:T(8,128)(2,1)S(1)} %copy-done.24), channel_id=1, replica_groups=mesh['dp'=8,'context'=4] {'context'}, dimensions={1}, use_global_device_ids=true | all-gather | bytes 491520 | tf_op jit(solution)/shard_map/all_gather | solution.py:88
  116.6 9.9 %collective-permute-done.2 = bf16[1,112,3072]{2,1,0:T(8,128)(2,1)S(1)} collective-permute-done((bf16[1,112,3072]{2,1,0:T(8,128)(2,1)S(1)}, bf16[1,112,3072]{2,1,0:T(8,128)(2,1)S(1)}, u32[]{:S(2)}, u32[]{:S(2)}) %collective-permute-start.2) | collective-permute-done | bytes 688160 | tf_op jit(solution)/shard_map/ppermute | solution.py:17
  142.6 26.6 %all-gather.15.cloned.1.call-done = bf16[3072,4,128]{2,1,0:T(4,128)(2,1)} async-done(((bf16[384,4,128]{2,1,0:T(4,128)(2,1)}), bf16[3072,4,128]{2,1,0:T(4,128)(2,1)}) %all-gather.15.cloned.1.call-update) | async-done | bytes 3145744 | tf_op jit(solution)/shard_map/all_gather | solution.py:93
  180.8 5.1 fusion.47
  185.9 43.8 %all-gather.7.cloned.1.call-done = bf16[3072,3,4,128]{3,2,1,0:T(4,128)(2,1)} async-done(((bf16[384,3,4,128]{3,2,1,0:T(4,128)(2,1)}), bf16[3072,3,4,128]{3,2,1,0:T(4,128)(2,1)}) %all-gather.7.cloned.1.call-update) | async-done | bytes 9437200 | tf_op jit(solution)/shard_map/all_gather | solution.py:92
  229.7 16.2 %reshape.239 = bf16[3072,1536]{1,0:T(8,128)(2,1)} reshape(bf16[3072,3,4,128]{3,2,1,0:T(4,128)(2,1)} %all-gather.7.cloned.1.call-done) | data formatting | bytes 18874368 | tf_op jit(solution)/shard_map/reshape | solution.py:97
  245.9 5.4 fusion.76
  251.2 38.9 %all-gather.11.cloned.1.call-done = bf16[3072,3,4,128]{3,2,1,0:T(4,128)(2,1)} async-done(((bf16[384,3,4,128]{3,2,1,0:T(4,128)(2,1)}), bf16[3072,3,4,128]{3,2,1,0:T(4,128)(2,1)}) %all-gather.11.cloned.1.call-update) | async-done | bytes 9437200 | tf_op jit(solution)/shard_map/all_gather | solution.py:91
  290.1 15.9 %reshape.240 = bf16[3072,1536]{1,0:T(8,128)(2,1)} reshape(bf16[3072,3,4,128]{3,2,1,0:T(4,128)(2,1)} %all-gather.11.cloned.1.call-done) | data formatting | bytes 18874368 | tf_op jit(solution)/shard_map/reshape | solution.py:96
  306.0 7.6 %fusion.21 = f32[448,1536]{1,0:T(8,128)S(1)} fusion(bf16[3072,1536]{1,0:T(8,128)(2,1)} %reshape.240, bf16[1,448,3072]{2,1,0:T(8,128)(2,1)S(1)} %copy-done.1, f32[3072]{0:T(1024)} %bitcast.218, f32[448]{0:T(512)} %add_rsqrt_fusion.2, f32[448]{0:T(512)S(1)} %broadcast_multiply_fusion.2, f32[3072]{0:T(1024)} %bitcast.216), kind=kOutput, calls=%fused_computation.37 | convolution fusion | flops 4236115968 | bytes 14970368 | tf_op jit(solution)/shard_map/dot_general | solution.py:105
  326.6 8.2 %fusion.44 = f32[512,4,128]{0,2,1:T(8,128)} fusion(f32[4,512,512]{1,2,0:T(8,128)} %fusion.78, f32[512,3,4,128]{0,3,2,1:T(8,128)S(1)} %bitcast.185, f32[512,4]{0,1:T(4,128)} %copy-done.30, f32[4,512,512]{1,2,0:T(8,128)} %copy-done.10, f32[4,512]{1,0:T(4,128)} %copy-done.35), kind=kOutput, calls=%fused_computation.56 | convolution fusion | flops 278399488 | bytes 18898944 | tf_op jit(solution)/shard_map/hij,ihe->jhe/dot_general | solution.py:168
  334.9 10.0 %multiply_reduce_fusion.3 = (f32[512,4]{0,1:T(4,128)}, f32[512,4]{0,1:T(4,128)}, f32[512,4,128]{0,2,1:T(8,128)}) fusion(f32[512,3,4,128]{0,3,2,1:T(8,128)S(1)} %bitcast.186, f32[512,4]{0,1:T(4,128)} %copy-done.30, f32[512,4,128]{0,2,1:T(8,128)} %fusion.44, f32[512,4]{0,1:T(4,128)} %copy-done.29, f32[4,512,512]{1,2,0:T(8,128)} %fusion.78, ...), kind=kOutput, calls=%fused_computation.72 | convolution fusion | flops 279968256 | bytes 22077440 | tf_op jit(solution)/shard_map/hij,jhe->ihe/dot_general | solution.py:167
  351.8 5.7 reshape.249
  357.5 5.8 %reshape.250 = bf16[3072,512,1]{1,0,2:T(8,128)(2,1)} reshape(bf16[3072,4,128]{2,1,0:T(4,128)(2,1)} %all-gather.15.cloned.1.call-done) | data formatting | bytes 6291456 | tf_op jit(solution)/shard_map/reshape | solution.py:98
  387.2 6.1 %convolution_convert_fusion = bf16[3072,1536]{0,1:T(8,128)(2,1)S(1)} fusion(bf16[448,1536]{0,1:T(8,128)(2,1)S(1)} %bitcast.205, bf16[1,448,3072]{2,1,0:T(8,128)(2,1)S(1)} %copy-done.2, f32[3072]{0:T(1024)S(1)} %bitcast.219, f32[448]{0:T(512)S(1)} %copy-done.38, f32[3072]{0:T(1024)S(1)} %bitcast.217, f32[448]{0:T(512)S(1)} %broadcast_multiply_fusion.2), kind=kOutput, calls=%fused_computation.3 | convolution fusion | flops 4240834560 | bytes 13594112 | tf_op jit(solution)/shard_map/dot_general | solution.py:49
  393.3 7.7 %pad_maximum_fusion = bf16[3072,2560]{0,1:T(8,128)(2,1)} fusion(bf16[3072,512]{0,1:T(8,128)(2,1)S(1)} %convolution_convert_fusion.2, bf16[3072,512]{0,1:T(8,128)(2,1)S(1)} %convolution_convert_fusion.3, bf16[3072,1536]{0,1:T(8,128)(2,1)S(1)} %convolution_convert_fusion), kind=kLoop, calls=%fused_computation.2 | loop fusion | flops 47185920 | bytes 31457280 | tf_op jit(solution)/shard_map/concatenate | solution.py:203
  401.0 19.2 %copy.92 = bf16[3072,2560]{1,0:T(8,128)(2,1)} copy(bf16[3072,2560]{0,1:T(8,128)(2,1)} %pad_maximum_fusion) | data formatting | bytes 31457280
  424.6 18.9 %reduce.2 = bf16[3072,64]{1,0:T(8,128)(2,1)} reduce(bf16[3072,1,64]{2,1,0:T(2,128)(2,1)} %bitcast.196, bf16[]{:T(256)} %broadcast.206), dimensions={1}, to_apply=%bitcast.155.reduce_sub_computation | reduce | bytes 786434
  446.2 12.6 %all_to_all.18 = bf16[8,2,12288]{2,1,0:T(2,128)(2,1)} all-to-all(bf16[8,2,12288]{2,1,0:T(2,128)(2,1)} %reshape.259), channel_id=1, replica_groups=mesh['dp'=8,'context'=4] {'dp'}, dimensions={0} | all-to-all | bytes 786432 | tf_op jit(solution)/shard_map/all_to_all | solution.py:207
  467.2 7.3 %fusion.101 = (bf16[3072]{0:T(1024)(128)(2,1)S(1)}, bf16[3072]{0:T(1024)(128)(2,1)S(1)}) fusion(f32[64]{0:T(128)} %copy-done.37, f32[64]{0:T(128)} %copy-done.36, bf16[1,64,3072]{2,1,0:T(8,128)(2,1)S(1)} %all_gather.24, bf16[64,1536]{0,1:T(8,128)(2,1)S(1)} %bitcast.199, bf16[3072,1536]{1,0:T(8,128)(2,1)} %reshape.239), kind=kOutput, calls=%fused_computation.133 | convolution fusion | flops 605153280 | bytes 10039808 | tf_op jit(solution)/shard_map/dot_general | solution.py:55
  474.6 9.5 %fusion.100 = (bf16[3072]{0:T(1024)(128)(2,1)S(1)}, bf16[3072]{0:T(1024)(128)(2,1)S(1)}) fusion(f32[448]{0:T(512)S(1)} %copy-done.39, f32[448]{0:T(512)S(1)} %broadcast_multiply_fusion.2, bf16[1,448,3072]{2,1,0:T(8,128)(2,1)S(1)} %copy-done.2, bf16[448,1536]{0,1:T(8,128)(2,1)S(1)} %bitcast.206, bf16[3072,1536]{1,0:T(8,128)(2,1)} %reshape.240), kind=kOutput, calls=%fused_computation.132 | convolution fusion | flops 4236109824 | bytes 13581824 | tf_op jit(solution)/shard_map/dot_general | solution.py:55
  494.7 20.3 %all-reduce = (bf16[1,3,3072]{2,0,1:T(2,128)(2,1)S(1)}, bf16[1,3,3072]{2,0,1:T(2,128)(2,1)S(1)}) all-reduce(bf16[1,3,3072]{2,0,1:T(2,128)(2,1)S(1)} %broadcast_in_dim.38, bf16[1,3,3072]{2,0,1:T(2,128)(2,1)S(1)} %broadcast_in_dim.40), channel_id=1, replica_groups=mesh['dp'=8,'context'=4] {'context'}, use_global_device_ids=true, to_apply=%region_16.17 | all-reduce | flops 18432 | bytes 73728 | tf_op jit(solution)/shard_map/psum | solution.py:196
  516.3 38.8 %reduce-scatter.7.cloned.1.call-done = bf16[384,2560]{1,0:T(8,128)(2,1)} async-done(((bf16[3072,2560]{1,0:T(8,128)(2,1)}), bf16[384,2560]{1,0:T(8,128)(2,1)}) %reduce-scatter.7.cloned.1.call-update) | async-done | bytes 1966096
  (185 shorter events, 128.3 us)
Async XLA Ops:
  7.2 101.4 %copy-start.27 = (bf16[1,3,3072]{2,1,0:T(4,128)(2,1)S(1)}, bf16[1,3,3072]{2,1,0:T(4,128)(2,1)}, u32[]{:S(2)}) copy-start(bf16[1,3,3072]{2,1,0:T(4,128)(2,1)} %param.12) | copy-start | bytes 55300
  7.2 102.0 %copy-start.28 = (bf16[1,3,3072]{2,1,0:T(4,128)(2,1)S(1)}, bf16[1,3,3072]{2,1,0:T(4,128)(2,1)}, u32[]{:S(2)}) copy-start(bf16[1,3,3072]{2,1,0:T(4,128)(2,1)} %param.13) | copy-start | bytes 55300
  7.2 83.7 %copy-start.24 = (bf16[1,16,3072]{2,1,0:T(8,128)(2,1)S(1)}, bf16[1,16,3072]{2,1,0:T(8,128)(2,1)}, u32[]{:S(2)}) copy-start(bf16[1,16,3072]{2,1,0:T(8,128)(2,1)} %param.19) | copy-start | bytes 294916
  7.2 120.2 %all-gather.9.cloned.1.call-start = ((), (), s32[]{:S(2)}) async-start(), calls=%async_computation.4 | async-start | bytes 3440640 | tf_op jit(solution)/shard_map/all_gather | solution.py:85
  7.9 103.9 %copy-start.14 = (bf16[1,112,3072]{2,1,0:T(8,128)(2,1)S(1)}, bf16[1,112,3072]{2,1,0:T(8,128)(2,1)}, u32[]{:S(2)}) copy-start(bf16[1,112,3072]{2,1,0:T(8,128)(2,1)} %param.18) | copy-start | bytes 2064388
  7.9 127.1 %all-gather.13.cloned.1.call-start = ((), (), s32[]{:S(2)}) async-start(), calls=%async_computation.6 | async-start | bytes 3538944 | tf_op jit(solution)/shard_map/all_gather | solution.py:94
  8.7 160.5 %all-gather.15.cloned.1.call-start = ((), (), s32[]{:S(2)}) async-start(), calls=%async_computation.7 | async-start | bytes 3538944 | tf_op jit(solution)/shard_map/all_gather | solution.py:93
  9.4 220.2 %all-gather.7.cloned.1.call-start = ((), (), s32[]{:S(2)}) async-start(), calls=%async_computation.3 | async-start | bytes 10616832 | tf_op jit(solution)/shard_map/all_gather | solution.py:92
  10.0 280.1 %all-gather.11.cloned.1.call-start = ((), (), s32[]{:S(2)}) async-start(), calls=%async_computation.5 | async-start | bytes 10616832 | tf_op jit(solution)/shard_map/all_gather | solution.py:91
  10.6 473.5 %all-gather.17.cloned.1.call-start = ((), (), s32[]{:S(2)}) async-start(), calls=%async_computation.9 | async-start | bytes 1769472 | tf_op jit(solution)/shard_map/all_gather | solution.py:208
  10.6 105.0 %collective-permute-start.1 = (bf16[1,112,3072]{2,1,0:T(8,128)(2,1)}, bf16[1,112,3072]{2,1,0:T(8,128)(2,1)S(1)}, u32[]{:S(2)}, u32[]{:S(2)}) collective-permute-start(bf16[1,112,3072]{2,1,0:T(8,128)(2,1)} %param.18), channel_id=1, source_target_pairs={{0,3},{1,0},{2,1},{3,2},{4,7},{5,4},{6,5},{7,6},{8,11},{9,8},{10,9... | collective-permute-start | bytes 2064392 | tf_op jit(solution)/shard_map/ppermute | solution.py:20
  15.8 97.9 %collective-permute-start = (bf16[1,112,3072]{2,1,0:T(8,128)(2,1)}, bf16[1,112,3072]{2,1,0:T(8,128)(2,1)S(1)}, u32[]{:S(2)}, u32[]{:S(2)}) collective-permute-start(bf16[1,112,3072]{2,1,0:T(8,128)(2,1)} %param.18), channel_id=1, source_target_pairs={{0,1},{1,2},{2,3},{3,0},{4,5},{5,6},{6,7},{7,4},{8,9},{9,10},{10,1... | collective-permute-start | bytes 2064392 | tf_op jit(solution)/shard_map/ppermute | solution.py:17
  90.6 23.1 %copy-start.36 = (f32[64]{0:T(128)}, f32[64]{0:T(128)S(1)}, u32[]{:S(2)}) copy-start(f32[64]{0:T(128)S(1)} %broadcast_multiply_fusion.3) | copy-start | bytes 772
  108.6 5.1 copy-start.37
  113.7 12.8 %collective-permute-start.2 = (bf16[1,112,3072]{2,1,0:T(8,128)(2,1)S(1)}, bf16[1,112,3072]{2,1,0:T(8,128)(2,1)S(1)}, u32[]{:S(2)}, u32[]{:S(2)}) collective-permute-start(bf16[1,112,3072]{2,1,0:T(8,128)(2,1)S(1)} %collective-permute-done), channel_id=1, source_target_pairs={{0,1},{1,2},{2,3},{3,0},{4,5},{5,6},{6,7},{7,4},{8,9},{9,10},{10,1... | collective-permute-start | bytes 2064392 | tf_op jit(solution)/shard_map/ppermute | solution.py:17
  185.9 60.0 %copy-start.4 = (bf16[1,64,3072]{2,1,0:T(8,128)(2,1)S(1)}, bf16[1,64,3072]{2,1,0:T(8,128)(2,1)}, u32[]{:S(2)}) copy-start(bf16[1,64,3072]{2,1,0:T(8,128)(2,1)} %fusion.61) | copy-start | bytes 1179652
  251.2 54.8 %copy-start.1 = (bf16[1,448,3072]{2,1,0:T(8,128)(2,1)S(1)}, bf16[1,448,3072]{2,1,0:T(8,128)(2,1)}, u32[]{:S(2)}) copy-start(bf16[1,448,3072]{2,1,0:T(8,128)(2,1)} %all-gather.9.cloned.1.call-done) | copy-start | bytes 8257540
  351.8 139.6 %reduce-scatter.5.cloned.1.call-start = ((), (), s32[]{:S(2)}) async-start(), calls=%async_computation.8 | async-start | bytes 3932160 | tf_op jit(solution)/shard_map/reduce_scatter | solution.py:134
  366.4 10.1 %copy-start.13 = (bf16[3072,512,1]{1,0,2:T(8,128)(2,1)S(1)}, bf16[3072,512,1]{1,0,2:T(8,128)(2,1)}, u32[]{:S(2)}) copy-start(bf16[3072,512,1]{1,0,2:T(8,128)(2,1)} %reshape.250) | copy-start | bytes 9437188
  381.3 173.9 %reduce-scatter.7.cloned.1.call-start = ((), (), s32[]{:S(2)}) async-start(), calls=%async_computation.10 | async-start | bytes 17694720
  443.5 23.7 %copy-start.11 = (bf16[64,3,4,128]{0,3,2,1:T(8,128)(2,1)S(1)}, bf16[64,3,4,128]{0,3,2,1:T(8,128)(2,1)}, u32[]{:S(2)}) copy-start(bf16[64,3,4,128]{0,3,2,1:T(8,128)(2,1)} %pad_maximum_fusion.5) | copy-start | bytes 589828
  467.2 7.4 %copy-start.21 = (bf16[448,3,4,128]{0,3,2,1:T(8,128)(2,1)S(1)}, bf16[448,3,4,128]{0,3,2,1:T(8,128)(2,1)}, u32[]{:S(2)}) copy-start(bf16[448,3,4,128]{0,3,2,1:T(8,128)(2,1)} %copy-done.20) | copy-start | bytes 4128772
  467.2 7.4 %copy-start.39 = (f32[448]{0:T(512)S(1)}, f32[448]{0:T(512)}, u32[]{:S(2)}) copy-start(f32[448]{0:T(512)} %add_rsqrt_fusion.2) | copy-start | bytes 5380
  474.6 9.6 %copy-start.19 = (bf16[1,64,8,384]{3,1,2,0:T(8,128)(2,1)S(1)}, bf16[1,64,8,384]{3,1,2,0:T(8,128)(2,1)}, u32[]{:S(2)}) copy-start(bf16[1,64,8,384]{3,1,2,0:T(8,128)(2,1)} %copy.74) | copy-start | bytes 1179652
  (27 other events, 75.5 us)
Sparse Core Ops, SparseCore 0:
  9.6 91.2 all-gather.8
  102.8 32.2 all-gather.12
  137.0 32.1 all-gather.14
  170.9 58.6 all-gather.6
  231.4 58.6 all-gather.10
  351.9 25.5 all-gather.16
  381.4 60.3 reduce-scatter.4
  445.3 109.7 reduce-scatter.6
